TPU v7x, 32 devices: a whole 2x2x4 slice. The times are simulated.
32 devices in a mesh: grp: 16 (over z, y, x), lag: 2 (over core).
Axes of the slice: x: 2, y: 2, z: 4, core: 2. Of those that a mesh axis runs over, the one named last changes fastest.
Arguments:
- waveforms: float32 [256, 8, 2048], P('grp'), may hold values from -6 to 6
- pair_bin: int32 [256, 256], P('grp'), may hold values from 0 to 127, as said below
Outputs:
- stack: float32 [128, 1024], P('grp', 'lag')
Inputs may be any that keep to these rules, and one draw needn't show every extreme that they name: pair_bin is symmetric: the bin of stations i and j is that of j and i.
All inputs are finite; a program needn't handle non-finite values.
Results may differ from a plain program's by a relative error of at most 0.0049.
Values may be sent and summed in bfloat16 or wider, within the bound.
No kernel may reach another device: no remote copies, remote signals or barrier semaphores. Data moves between devices by JAX's collectives and lax.ppermute only.
A program may use at most 64 MiB of HBM per device.

v0:
```python
import math
import jax
import jax.numpy as jnp
from jax import lax
from jax.sharding import PartitionSpec as P

NFFT = 2048
LAGS = 1024
HW = 32
BIN_DEV = 8
EPSILON = 1e-06


def with_halo(block, sides, width):
    for axis, dim in sides:
        count = lax.axis_size(axis)
        forward = [(i, i + 1) for i in range(count - 1)]
        backward = [(target, source) for source, target in forward]
        low = lax.ppermute(
            lax.slice_in_dim(block, block.shape[dim] - width, None, axis=dim), axis, forward
        )
        high = lax.ppermute(lax.slice_in_dim(block, 0, width, axis=dim), axis, backward)
        block = jnp.concatenate([low, block, high], axis=dim)
    return block


def forward_table(freq_start, freq_count):
    sample_index = jnp.arange(NFFT, dtype=jnp.int32)[:, None]
    bin_index = freq_start + jnp.arange(freq_count, dtype=jnp.int32)[None, :]
    phase = (sample_index * bin_index % NFFT).astype(jnp.float32) * (2.0 * math.pi / NFFT)
    return jnp.concatenate([jnp.cos(phase), -jnp.sin(phase)], axis=1)


def inverse_table(freq_start, freq_count):
    bin_index = freq_start + jnp.arange(freq_count, dtype=jnp.int32)
    shifted = jnp.arange(LAGS, dtype=jnp.int32) - LAGS // 2
    phase = (bin_index[:, None] * shifted[None, :] % NFFT).astype(jnp.float32) * (
        2.0 * math.pi / NFFT
    )
    weight = jnp.where(bin_index == 0, 1.0, 2.0).astype(jnp.float32)[:, None] / NFFT
    return jnp.concatenate([weight * jnp.cos(phase), -weight * jnp.sin(phase)], axis=0)


def window_band(freq_count):
    padded_index = jnp.arange(freq_count + 2 * HW, dtype=jnp.int32)[:, None]
    bin_index = jnp.arange(freq_count, dtype=jnp.int32)[None, :]
    inside = (padded_index >= bin_index) & (padded_index <= bin_index + 2 * HW)
    return inside.astype(jnp.float32)


def window_count(freq_start, freq_count, half_length):
    bin_index = freq_start + jnp.arange(freq_count, dtype=jnp.int32)
    upper = jnp.minimum(bin_index + HW, half_length - 1)
    lower = jnp.maximum(bin_index - HW, 0)
    return (upper - lower + 1).astype(jnp.float32)


def add_block(running, whitened, remote, column_start, keep_pairs, imag_sign, pair_bin):
    freq_count = whitened.shape[2] // 2
    row_count = whitened.shape[0]
    column_count = remote.shape[0]
    own_real = whitened[..., :freq_count]
    own_imag = whitened[..., freq_count:]
    far_real = remote[..., :freq_count]
    far_imag = remote[..., freq_count:]
    own_stack = jnp.concatenate([own_real, own_imag], axis=1)
    own_alt = jnp.concatenate([own_real, -own_imag], axis=1)
    far_stack = jnp.concatenate([far_real, far_imag], axis=1)
    far_alt = jnp.concatenate([far_imag, far_real], axis=1)
    real_sum = jnp.einsum("asf,bsf->abf", own_stack, far_stack, preferred_element_type=jnp.float32)
    imag_sum = (
        jnp.einsum("asf,bsf->abf", own_alt, far_alt, preferred_element_type=jnp.float32) * imag_sign
    )
    cross = jnp.concatenate([real_sum, imag_sum], axis=2).astype(jnp.bfloat16)
    cross = cross.reshape(row_count * column_count, 2 * freq_count)
    block_bins = lax.dynamic_slice_in_dim(pair_bin, column_start, column_count, 1)
    block_bins = jnp.where(keep_pairs, block_bins, -1).reshape(-1)
    onehot = (block_bins[None, :] == jnp.arange(running.shape[0], dtype=jnp.int32)[:, None]).astype(
        jnp.bfloat16
    )
    return running + jnp.dot(onehot, cross, preferred_element_type=jnp.float32)


def local(waveforms, pair_bin):
    station_count = waveforms.shape[0]
    segments = waveforms.shape[1]
    groups = lax.axis_size("grp")
    group_index = lax.axis_index("grp")
    half_length = NFFT // 2
    freq_count = half_length // lax.axis_size("lag")
    freq_start = lax.axis_index("lag") * freq_count
    spectra = jnp.dot(
        waveforms.reshape(station_count * segments, NFFT),
        forward_table(freq_start, freq_count),
        precision=lax.Precision.HIGHEST,
        preferred_element_type=jnp.float32,
    )
    spectra = spectra.reshape(station_count, segments, 2 * freq_count)
    real_part = spectra[..., :freq_count]
    imag_part = spectra[..., freq_count:]
    amplitude = jnp.sqrt(real_part * real_part + imag_part * imag_part)
    padded = with_halo(amplitude, (("lag", 2),), HW)
    smoothed = jnp.dot(
        padded.reshape(station_count * segments, freq_count + 2 * HW),
        window_band(freq_count),
        precision=lax.Precision.HIGHEST,
        preferred_element_type=jnp.float32,
    )
    smoothed = smoothed.reshape(station_count, segments, freq_count) / window_count(
        freq_start, freq_count, half_length
    )
    whitened = jnp.concatenate(
        [real_part / (smoothed + EPSILON), imag_part / (smoothed + EPSILON)], axis=2
    ).astype(jnp.bfloat16)
    bins_total = BIN_DEV * groups
    row_start = group_index * station_count
    initial = jnp.zeros((bins_total, 2 * freq_count), jnp.float32)
    local_rows = jnp.arange(station_count, dtype=jnp.int32)
    remote = lax.all_gather(whitened, "grp", axis=0, tiled=True)
    group_total = remote.shape[0] // station_count
    per_step = max((divisor for divisor in (4, 3, 2, 1) if group_total % divisor == 0))
    step_count = group_total // per_step
    block_width = per_step * station_count
    blocks = remote.reshape(step_count, block_width, remote.shape[1], remote.shape[2])

    def one_step(step_index, carried):
        column_block = lax.dynamic_index_in_dim(blocks, step_index, 0, keepdims=False)
        column_start = step_index * block_width
        column_index = column_start + jnp.arange(block_width, dtype=jnp.int32)
        keep_pairs = column_index[None, :] > (row_start + local_rows)[:, None]

        def compute(accumulated):
            return add_block(
                accumulated, whitened, column_block, column_start, keep_pairs, 1.0, pair_bin
            )

        return lax.cond(
            column_start + block_width > row_start,
            compute,
            lambda accumulated: accumulated,
            carried,
        )

    binned = lax.fori_loop(0, step_count, one_step, initial)
    inverse = inverse_table(freq_start, freq_count)
    owned_bins = lax.psum_scatter(binned, "grp", scatter_dimension=0, tiled=True)
    lag_partial = jnp.dot(
        owned_bins, inverse, precision=lax.Precision.HIGHEST, preferred_element_type=jnp.float32
    )
    return lax.psum_scatter(lag_partial, "lag", scatter_dimension=1, tiled=True)


def solution(mesh):
    in_specs = (P("grp", None, None), P("grp", None))
    out_specs = P("grp", "lag")
    return jax.shard_map(local, mesh=mesh, in_specs=in_specs, out_specs=out_specs, check_vma=False)
```

profile of v0, /device:TPU:0, one launch (start us, length us, event | category | flops | bytes accessed | tf_op | source)
XLA Modules:
  0.0 322.4 jit_solution(7806394600709355711)
XLA Ops:
  6.5 16.7 %fusion.42 = (f32[2048,512]{1,0:T(8,128)S(1)}, f32[2048,512]{1,0:T(8,128)S(1)}) fusion(s32[512]{0:T(512)S(1)} %iota_add_fusion.2), kind=kLoop, calls=%fused_computation.56 | loop fusion | flops 15728640 | bytes 8390656 | tf_op jit(solution)/shard_map/cos | solution.py:31
  23.2 4.7 %fusion.43 = f32[16,8,1024]{2,1,0:T(8,128)S(1)} fusion(f32[2048,512]{1,0:T(8,128)S(1)} %get-tuple-element.295, f32[2048,512]{1,0:T(8,128)S(1)} %get-tuple-element.294, f32[16,8,2048]{2,1,0:T(8,128)S(1)} %copy-done), kind=kOutput, calls=%fused_computation.59 | convolution fusion | flops 3223322624 | bytes 9961472 | tf_op jit(solution)/shard_map/dot_general | solution.py:92
  28.1 2.4 collective-permute-start
  30.5 1.3 collective-permute-start.1
  31.8 1.8 collective-permute-done.1
  35.1 78.3 %all-gather.2.cloned.1.call-done = bf16[256,8,1024]{2,1,0:T(8,128)(2,1)} async-done(((bf16[16,8,1024]{2,1,0:T(8,128)(2,1)}), bf16[256,8,1024]{2,1,0:T(8,128)(2,1)}) %all-gather.2.cloned.1.call-update) | async-done | bytes 4194320 | tf_op jit(solution)/shard_map/all_gather | solution.py:119
  113.4 11.8 %copy.13 = bf16[4,64,8,1024]{1,2,3,0:T(8,128)(2,1)} copy(bf16[4,64,8,1024]{3,2,1,0:T(8,128)(2,1)} %bitcast.32) | data formatting | bytes 8388608
  126.0 107.5 %while.17 = (s32[]{:T(128)}, f32[128,1024]{1,0:T(8,128)}, s32[]{:T(128)}, s32[16,256]{1,0:T(8,128)S(1)}, bf16[4,64,8,1024]{1,2,3,0:T(8,128)(2,1)}, /*index=5*/bf16[16,8,1024]{2,1,0:T(8,128)(2,1)}, s32[]{:T(128)}, s32[]{:T(128)}) while((s32[]{:T(128)}, f32[128,1024]{1,0:T(8,128)}, s32[]{:T(128)}, s32[16,256]{1,0:T(8,128)S(1)}, ...), condition=%wide.region_3.4_spmd.clone, body=%wide.region_0.3_spmd.clone.sunk | while | flops 312674400 | bytes 23090748 | solution.py:144
  126.0 26.9 %conditional.3 = (f32[128,1024]{1,0:T(8,128)}) conditional(s32[]{:T(128)} %convert_element_type.47, f32[128,1024]{1,0:T(8,128)} %get-tuple-element.346, (s32[]{:T(128)}, s32[1,64]{1,0:T(1,128)S(1)}, s32[]{:T(128)}, s32[16]{0:T(128)S(1)}, s32[16,256]{1,0:T(8,128)S(1)}, /*index=5*/s32[]{:T(128)}, bf16[4,64,8,1024]{1,2,3,0:T(8,128)(2,1)}, ...), branch_computations={%region_1.1_spmd, %region_2.2_spmd} | conditional | flops 312674400 | bytes 23090232 | solution.py:137
  126.1 1.7 dynamic-slice_bitcast_fusion
  129.7 3.7 %copy.9 = bf16[16,16,512]{1,0,2:T(8,128)(2,1)} copy(bf16[16,16,512]{2,1,0:T(8,128)(2,1)} %get-tuple-element.286) | data formatting | bytes 524288 | tf_op jit(solution)/shard_map/while/body/eval_jaxpr/cond/branch_1_fun/concatenate | solution.py:66
  133.4 4.2 %convert_bitcast_fusion.1 = bf16[16,64,512]{1,0,2:T(8,128)(2,1)} fusion(bf16[16,16,512]{1,0,2:T(8,128)(2,1)} %copy.9, bf16[64,8,512]{0,1,2:T(8,128)(2,1)S(1)} %get-tuple-element.281, bf16[64,8,512]{0,1,2:T(8,128)(2,1)S(1)} %get-tuple-element.282), kind=kOutput, calls=%fused_computation.14 | convolution fusion | flops 19398656 | bytes 2359296 | tf_op jit(solution)/shard_map/while/body/eval_jaxpr/cond/branch_1_fun/asf,bsf->abf/dot_general | solution.py:70
  137.5 3.3 %copy.10 = bf16[16,64,512]{2,1,0:T(8,128)(2,1)} copy(bf16[16,64,512]{1,0,2:T(8,128)(2,1)} %convert_bitcast_fusion.1) | data formatting | bytes 2097152 | tf_op jit(solution)/shard_map/while/body/eval_jaxpr/cond/branch_1_fun/asf,bsf->abf/transpose | solution.py:70
  140.9 2.8 copy.11
  143.7 4.2 %convert_bitcast_fusion = bf16[16,64,512]{1,0,2:T(8,128)(2,1)} fusion(bf16[16,16,512]{1,0,2:T(8,128)(2,1)} %copy.11, bf16[64,8,512]{0,1,2:T(8,128)(2,1)S(1)} %get-tuple-element.282, bf16[64,8,512]{0,1,2:T(8,128)(2,1)S(1)} %get-tuple-element.281), kind=kOutput, calls=%fused_computation.13 | convolution fusion | flops 19398656 | bytes 2359296 | tf_op jit(solution)/shard_map/while/body/eval_jaxpr/cond/branch_1_fun/asf,bsf->abf/dot_general | solution.py:72
  147.8 2.6 copy.12
  150.6 2.3 fusion.18
  152.9 26.9 %conditional.3 = (f32[128,1024]{1,0:T(8,128)}) conditional(s32[]{:T(128)} %convert_element_type.47, f32[128,1024]{1,0:T(8,128)} %get-tuple-element.346, (s32[]{:T(128)}, s32[1,64]{1,0:T(1,128)S(1)}, s32[]{:T(128)}, s32[16]{0:T(128)S(1)}, s32[16,256]{1,0:T(8,128)S(1)}, /*index=5*/s32[]{:T(128)}, bf16[4,64,8,1024]{1,2,3,0:T(8,128)(2,1)}, ...), branch_computations={%region_1.1_spmd, %region_2.2_spmd} | conditional | flops 312674400 | bytes 23090232 | solution.py:137
  152.9 1.7 dynamic-slice_bitcast_fusion
  156.6 3.7 %copy.9 = bf16[16,16,512]{1,0,2:T(8,128)(2,1)} copy(bf16[16,16,512]{2,1,0:T(8,128)(2,1)} %get-tuple-element.286) | data formatting | bytes 524288 | tf_op jit(solution)/shard_map/while/body/eval_jaxpr/cond/branch_1_fun/concatenate | solution.py:66
  160.2 4.2 %convert_bitcast_fusion.1 = bf16[16,64,512]{1,0,2:T(8,128)(2,1)} fusion(bf16[16,16,512]{1,0,2:T(8,128)(2,1)} %copy.9, bf16[64,8,512]{0,1,2:T(8,128)(2,1)S(1)} %get-tuple-element.281, bf16[64,8,512]{0,1,2:T(8,128)(2,1)S(1)} %get-tuple-element.282), kind=kOutput, calls=%fused_computation.14 | convolution fusion | flops 19398656 | bytes 2359296 | tf_op jit(solution)/shard_map/while/body/eval_jaxpr/cond/branch_1_fun/asf,bsf->abf/dot_general | solution.py:70
  164.4 3.3 %copy.10 = bf16[16,64,512]{2,1,0:T(8,128)(2,1)} copy(bf16[16,64,512]{1,0,2:T(8,128)(2,1)} %convert_bitcast_fusion.1) | data formatting | bytes 2097152 | tf_op jit(solution)/shard_map/while/body/eval_jaxpr/cond/branch_1_fun/asf,bsf->abf/transpose | solution.py:70
  167.7 2.8 copy.11
  170.5 4.2 %convert_bitcast_fusion = bf16[16,64,512]{1,0,2:T(8,128)(2,1)} fusion(bf16[16,16,512]{1,0,2:T(8,128)(2,1)} %copy.11, bf16[64,8,512]{0,1,2:T(8,128)(2,1)S(1)} %get-tuple-element.282, bf16[64,8,512]{0,1,2:T(8,128)(2,1)S(1)} %get-tuple-element.281), kind=kOutput, calls=%fused_computation.13 | convolution fusion | flops 19398656 | bytes 2359296 | tf_op jit(solution)/shard_map/while/body/eval_jaxpr/cond/branch_1_fun/asf,bsf->abf/dot_general | solution.py:72
  174.7 2.6 copy.12
  177.5 2.3 fusion.18
  179.8 26.9 %conditional.3 = (f32[128,1024]{1,0:T(8,128)}) conditional(s32[]{:T(128)} %convert_element_type.47, f32[128,1024]{1,0:T(8,128)} %get-tuple-element.346, (s32[]{:T(128)}, s32[1,64]{1,0:T(1,128)S(1)}, s32[]{:T(128)}, s32[16]{0:T(128)S(1)}, s32[16,256]{1,0:T(8,128)S(1)}, /*index=5*/s32[]{:T(128)}, bf16[4,64,8,1024]{1,2,3,0:T(8,128)(2,1)}, ...), branch_computations={%region_1.1_spmd, %region_2.2_spmd} | conditional | flops 312674400 | bytes 23090232 | solution.py:137
  179.8 1.7 dynamic-slice_bitcast_fusion
  183.4 3.7 %copy.9 = bf16[16,16,512]{1,0,2:T(8,128)(2,1)} copy(bf16[16,16,512]{2,1,0:T(8,128)(2,1)} %get-tuple-element.286) | data formatting | bytes 524288 | tf_op jit(solution)/shard_map/while/body/eval_jaxpr/cond/branch_1_fun/concatenate | solution.py:66
  187.1 4.2 %convert_bitcast_fusion.1 = bf16[16,64,512]{1,0,2:T(8,128)(2,1)} fusion(bf16[16,16,512]{1,0,2:T(8,128)(2,1)} %copy.9, bf16[64,8,512]{0,1,2:T(8,128)(2,1)S(1)} %get-tuple-element.281, bf16[64,8,512]{0,1,2:T(8,128)(2,1)S(1)} %get-tuple-element.282), kind=kOutput, calls=%fused_computation.14 | convolution fusion | flops 19398656 | bytes 2359296 | tf_op jit(solution)/shard_map/while/body/eval_jaxpr/cond/branch_1_fun/asf,bsf->abf/dot_general | solution.py:70
  191.3 3.3 %copy.10 = bf16[16,64,512]{2,1,0:T(8,128)(2,1)} copy(bf16[16,64,512]{1,0,2:T(8,128)(2,1)} %convert_bitcast_fusion.1) | data formatting | bytes 2097152 | tf_op jit(solution)/shard_map/while/body/eval_jaxpr/cond/branch_1_fun/asf,bsf->abf/transpose | solution.py:70
  194.6 2.8 copy.11
  197.4 4.2 %convert_bitcast_fusion = bf16[16,64,512]{1,0,2:T(8,128)(2,1)} fusion(bf16[16,16,512]{1,0,2:T(8,128)(2,1)} %copy.11, bf16[64,8,512]{0,1,2:T(8,128)(2,1)S(1)} %get-tuple-element.282, bf16[64,8,512]{0,1,2:T(8,128)(2,1)S(1)} %get-tuple-element.281), kind=kOutput, calls=%fused_computation.13 | convolution fusion | flops 19398656 | bytes 2359296 | tf_op jit(solution)/shard_map/while/body/eval_jaxpr/cond/branch_1_fun/asf,bsf->abf/dot_general | solution.py:72
  201.6 2.6 copy.12
  204.4 2.3 fusion.18
  206.7 26.9 %conditional.3 = (f32[128,1024]{1,0:T(8,128)}) conditional(s32[]{:T(128)} %convert_element_type.47, f32[128,1024]{1,0:T(8,128)} %get-tuple-element.346, (s32[]{:T(128)}, s32[1,64]{1,0:T(1,128)S(1)}, s32[]{:T(128)}, s32[16]{0:T(128)S(1)}, s32[16,256]{1,0:T(8,128)S(1)}, /*index=5*/s32[]{:T(128)}, bf16[4,64,8,1024]{1,2,3,0:T(8,128)(2,1)}, ...), branch_computations={%region_1.1_spmd, %region_2.2_spmd} | conditional | flops 312674400 | bytes 23090232 | solution.py:137
  206.7 1.7 dynamic-slice_bitcast_fusion
  210.3 3.7 %copy.9 = bf16[16,16,512]{1,0,2:T(8,128)(2,1)} copy(bf16[16,16,512]{2,1,0:T(8,128)(2,1)} %get-tuple-element.286) | data formatting | bytes 524288 | tf_op jit(solution)/shard_map/while/body/eval_jaxpr/cond/branch_1_fun/concatenate | solution.py:66
  214.0 4.2 %convert_bitcast_fusion.1 = bf16[16,64,512]{1,0,2:T(8,128)(2,1)} fusion(bf16[16,16,512]{1,0,2:T(8,128)(2,1)} %copy.9, bf16[64,8,512]{0,1,2:T(8,128)(2,1)S(1)} %get-tuple-element.281, bf16[64,8,512]{0,1,2:T(8,128)(2,1)S(1)} %get-tuple-element.282), kind=kOutput, calls=%fused_computation.14 | convolution fusion | flops 19398656 | bytes 2359296 | tf_op jit(solution)/shard_map/while/body/eval_jaxpr/cond/branch_1_fun/asf,bsf->abf/dot_general | solution.py:70
  218.1 3.3 %copy.10 = bf16[16,64,512]{2,1,0:T(8,128)(2,1)} copy(bf16[16,64,512]{1,0,2:T(8,128)(2,1)} %convert_bitcast_fusion.1) | data formatting | bytes 2097152 | tf_op jit(solution)/shard_map/while/body/eval_jaxpr/cond/branch_1_fun/asf,bsf->abf/transpose | solution.py:70
  221.5 2.8 copy.11
  224.3 4.2 %convert_bitcast_fusion = bf16[16,64,512]{1,0,2:T(8,128)(2,1)} fusion(bf16[16,16,512]{1,0,2:T(8,128)(2,1)} %copy.11, bf16[64,8,512]{0,1,2:T(8,128)(2,1)S(1)} %get-tuple-element.282, bf16[64,8,512]{0,1,2:T(8,128)(2,1)S(1)} %get-tuple-element.281), kind=kOutput, calls=%fused_computation.13 | convolution fusion | flops 19398656 | bytes 2359296 | tf_op jit(solution)/shard_map/while/body/eval_jaxpr/cond/branch_1_fun/asf,bsf->abf/dot_general | solution.py:72
  228.4 2.6 copy.12
  231.2 2.3 fusion.18
  233.6 9.8 %cosine_multiply_fusion = (f32[512,1024]{1,0:T(8,128)S(1)}, f32[512,1024]{1,0:T(8,128)}) fusion(s32[1024]{0:T(1024)S(1)} %iota_add_fusion, s32[512]{0:T(512)S(1)} %iota_add_fusion.2, f32[512]{0:T(512)S(1)} %get-tuple-element.296, f32[512]{0:T(512)S(1)} %get-tuple-element.297), kind=kLoop, calls=%fused_computation.55 | loop fusion | flops 8388608 | bytes 4204544 | tf_op jit(solution)/shard_map/mul | solution.py:41
  243.4 64.2 %reduce-scatter.3.cloned.1.call-done = f32[8,1024]{1,0:T(8,128)} async-done(((f32[128,1024]{1,0:T(8,128)}), f32[8,1024]{1,0:T(8,128)}) %reduce-scatter.3.cloned.1.call-update) | async-done | bytes 32784 | tf_op jit(solution)/shard_map/reduce_scatter | solution.py:146
  307.6 4.3 %fusion.32 = f32[8,1024]{1,0:T(8,128)} fusion(f32[8,1024]{1,0:T(8,128)} %reduce-scatter.3.cloned.1.call-done, f32[512,1024]{1,0:T(8,128)} %get-tuple-element.293, f32[512,1024]{1,0:T(8,128)S(1)} %get-tuple-element.292), kind=kOutput, calls=%fused_computation.38 | convolution fusion | flops 101711872 | bytes 4259840 | tf_op jit(solution)/shard_map/dot_general | solution.py:147
  311.9 3.9 %reduce-scatter.5.cloned.1.call-done = f32[8,512]{1,0:T(8,128)} async-done(((f32[8,1024]{1,0:T(8,128)}), f32[8,512]{1,0:T(8,128)}) %reduce-scatter.5.cloned.1.call-update) | async-done | bytes 16400 | tf_op jit(solution)/shard_map/reduce_scatter | solution.py:150
  (64 shorter events, 10.8 us)
Async XLA Ops:
  6.5 16.7 %copy-start = (f32[16,8,2048]{2,1,0:T(8,128)S(1)}, f32[16,8,2048]{2,1,0:T(8,128)}, u32[]{:S(2)}) copy-start(f32[16,8,2048]{2,1,0:T(8,128)} %param.6) | copy-start | bytes 3145732
  6.5 106.8 %all-gather.2.cloned.1.call-start = ((), (), s32[]{:S(2)}) async-start(), calls=%async_computation.2 | async-start | bytes 4456448 | tf_op jit(solution)/shard_map/all_gather | solution.py:119
  28.1 3.7 %collective-permute-start = (f32[16,8,32]{2,1,0:T(8,128)S(1)}, f32[16,8,32]{2,1,0:T(8,128)S(1)}, u32[]{:S(2)}, u32[]{:S(2)}) collective-permute-start(f32[16,8,32]{2,1,0:T(8,128)S(1)} %get-tuple-element.290), channel_id=1, source_target_pairs={{0,1},{2,3},{4,5},{6,7},{8,9},{10,11},{12,13},{14,15},{16,17},{18,... | collective-permute-start | bytes 49160 | tf_op jit(solution)/shard_map/ppermute | solution.py:19
  30.5 3.1 collective-permute-start.1
  35.0 272.5 %reduce-scatter.3.cloned.1.call-start = ((), (), s32[]{:S(2)}) async-start(), calls=%async_computation.3 | async-start | bytes 557056 | tf_op jit(solution)/shard_map/reduce_scatter | solution.py:146
  113.3 12.7 %copy-start.2 = (s32[16,256]{1,0:T(8,128)S(1)}, s32[16,256]{1,0:T(8,128)}, u32[]{:S(2)}) copy-start(s32[16,256]{1,0:T(8,128)} %param.7) | copy-start | bytes 49156
  147.8 2.8 copy-start.1
  174.7 2.8 copy-start.1
  201.6 2.8 copy-start.1
  228.4 2.8 copy-start.1
  233.5 82.3 %reduce-scatter.5.cloned.1.call-start = ((), (), s32[]{:S(2)}) async-start(), calls=%async_computation.4 | async-start | bytes 49152 | tf_op jit(solution)/shard_map/reduce_scatter | solution.py:150
Sparse Core Ops, SparseCore 0:
  35.2 78.1 all-gather.1
  233.7 73.8 reduce-scatter.2
  312.0 3.7 reduce-scatter.4
where the time goes:
time: 324 us; the launch traced here: 322 us
  waiting for transfers between devices  148 us (46%)
  local copies, waits for them, and re-layouts  70.2 us (22%)
  matrix products  52.1 us (16%)
  other arithmetic  34.7 us (11%)
  between operations  13.2 us (4%)
  starting transfers between devices  3.73 us (1%)
    all_gather x1, waiting for transfers between devices, local(): remote = lax.all_gather(whitened, 'grp', axis=0, tiled=True)  78.3 us
    reduce_scatter x1, waiting for transfers between devices, local(): lax.psum_scatter(binned, 'grp', scatter_dimension=0, tiled=True)  64.2 us
    cos x1, other arithmetic, forward_table(): return jnp.concatenate([jnp.cos(phase), -jnp.sin(phase)], axis=1)  16.7 us
    dot_general x4, matrix products, add_block(): jnp.einsum('asf,bsf->abf', own_alt, far_alt, preferred_element_type=jnp.f...  16.6 us
    dot_general x4, matrix products, add_block(): jnp.einsum('asf,bsf->abf', own_stack, far_stack, preferred_element_type=j...  16.6 us
    concatenate x4, local copies, waits for them, and re-layouts, add_block(): own_stack = jnp.concatenate([own_real, own_imag], axis=1)  14.7 us
    transpose x4, local copies, waits for them, and re-layouts, add_block(): jnp.einsum('asf,bsf->abf', own_stack, far_stack, preferred_element_type=j...  13.3 us
    unnamed x5, local copies, waits for them, and re-layouts  11.8 us
  transfers between devices with their start and end apart: 5, of which 4 were waited for; matrix products, arithmetic and copies ran while one was open for 3% of the time, Pallas kernels for 0%

commit v1 on v0

--- a/solution.py
+++ b/solution.py
@@ -9,6 +9,35 @@
 HW = 32
 BIN_DEV = 8
 EPSILON = 1e-06
+
+
+def _pair_samples(mesh_ax, content):
+    local_now = lax.axis_size(mesh_ax)
+    plain = lax.axis_index(mesh_ax)
+    w2, res, out_arr = (local_now, plain, content.shape[0])
+    copies = []
+    for jj, p in enumerate(content.shape):
+        copies.append(p * w2 if jj == 0 else p)
+    shaped = jnp.zeros(copies, content.dtype)
+    response = lax.dynamic_update_slice_in_dim(shaped, content, res * out_arr, axis=0)
+    step_out = reply = content
+    for nth in range(1, w2 // 2 + 1):
+        views = []
+        for jj in range(w2):
+            views.append((jj, (jj + 1) % w2))
+        step_out = lax.ppermute(step_out, mesh_ax, views)
+        response = lax.dynamic_update_slice_in_dim(
+            response, step_out, (res - nth) % w2 * out_arr, axis=0
+        )
+        if 2 * nth < w2:
+            inbox = []
+            for jj in range(w2):
+                inbox.append((jj, (jj - 1) % w2))
+            reply = lax.ppermute(reply, mesh_ax, inbox)
+            response = lax.dynamic_update_slice_in_dim(
+                response, reply, (res + nth) % w2 * out_arr, axis=0
+            )
+    return response
 
 
 def with_halo(block, sides, width):
@@ -116,7 +145,7 @@
     row_start = group_index * station_count
     initial = jnp.zeros((bins_total, 2 * freq_count), jnp.float32)
     local_rows = jnp.arange(station_count, dtype=jnp.int32)
-    remote = lax.all_gather(whitened, "grp", axis=0, tiled=True)
+    remote = _pair_samples("grp", whitened)
     group_total = remote.shape[0] // station_count
     per_step = max((divisor for divisor in (4, 3, 2, 1) if group_total % divisor == 0))
     step_count = group_total // per_step

time: 324 us -> 353 us (1.090)
  starting transfers between devices: 3.73 us -> 46.9 us
  waiting for transfers between devices: 148 us -> 120 us
  local copies, waits for them, and re-layouts: 70.2 us -> 83.2 us
    all_gather x1 -> x0, waiting for transfers between devices: 78.3 us -> none  [local(): remote = lax.all_gather(whitened, 'grp', axis=0, tiled=True)]
    ppermute x0 -> x15, waiting for transfers between devices: none -> 51.1 us  [the longest x8 51.1 us: _pair_samples(): step_out = lax.ppermute(step_out, mesh_ax, views)]
    ppermute x0 -> x15, starting transfers between devices: none -> 43.2 us  [the longest x7 23.7 us: _pair_samples(): reply = lax.ppermute(reply, mesh_ax, inbox)]
    dynamic_update_slice x0 -> x15, local copies, waits for them, and re-layouts: none -> 10.9 us  [the longest x8 5.78 us: _pair_samples(): lax.dynamic_update_slice_in_dim(response, step_out, (res - nth) % w2 * ou...]
  transfers between devices with their start and end apart: 5 -> 19, of which waited for: 4 -> 11; matrix products, arithmetic and copies ran while one was open for 3% -> 6% of each run, Pallas kernels for 0% -> 0%
where the time goes in v1:
time: 353 us; the launch traced here: 352 us
  waiting for transfers between devices  120 us (34%)
  local copies, waits for them, and re-layouts  83.2 us (24%)
  matrix products  53.5 us (15%)
  starting transfers between devices  46.9 us (13%)
  other arithmetic  34.9 us (10%)
  between operations  13.5 us (4%)
    reduce_scatter x1, waiting for transfers between devices, local(): lax.psum_scatter(binned, 'grp', scatter_dimension=0, tiled=True)  62.8 us
    ppermute x8, waiting for transfers between devices, _pair_samples(): step_out = lax.ppermute(step_out, mesh_ax, views)  51.1 us
    ppermute x7, starting transfers between devices, _pair_samples(): reply = lax.ppermute(reply, mesh_ax, inbox)  23.7 us
    ppermute x8, starting transfers between devices, _pair_samples(): step_out = lax.ppermute(step_out, mesh_ax, views)  19.6 us
    dot_general x4, matrix products, add_block(): jnp.einsum('asf,bsf->abf', own_alt, far_alt, preferred_element_type=jnp.f...  16.7 us
    dot_general x4, matrix products, add_block(): jnp.einsum('asf,bsf->abf', own_stack, far_stack, preferred_element_type=j...  16.7 us
    cos x1, other arithmetic, forward_table(): return jnp.concatenate([jnp.cos(phase), -jnp.sin(phase)], axis=1)  16.7 us
    concatenate x4, local copies, waits for them, and re-layouts, add_block(): own_stack = jnp.concatenate([own_real, own_imag], axis=1)  14.7 us
  transfers between devices with their start and end apart: 19, of which 11 were waited for; matrix products, arithmetic and copies ran while one was open for 6% of the time, Pallas kernels for 0%

profile of v1, /device:TPU:0, one launch (start us, length us, event | category | flops | bytes accessed | tf_op | source)
XLA Modules:
  0.0 351.9 jit_solution(7420434710235856762)
XLA Ops:
  6.5 16.7 %fusion.42 = (f32[2048,512]{1,0:T(8,128)S(1)}, f32[2048,512]{1,0:T(8,128)S(1)}) fusion(s32[512]{0:T(512)S(1)} %iota_add_fusion.2), kind=kLoop, calls=%fused_computation.56 | loop fusion | flops 15728640 | bytes 8390656 | tf_op jit(solution)/shard_map/cos | solution.py:60
  23.2 4.7 %fusion.43 = f32[16,8,1024]{2,1,0:T(8,128)S(1)} fusion(f32[2048,512]{1,0:T(8,128)S(1)} %get-tuple-element.297, f32[2048,512]{1,0:T(8,128)S(1)} %get-tuple-element.296, f32[16,8,2048]{2,1,0:T(8,128)S(1)} %copy-done), kind=kOutput, calls=%fused_computation.59 | convolution fusion | flops 3223322624 | bytes 9961472 | tf_op jit(solution)/shard_map/dot_general | solution.py:121
  40.0 4.0 %collective-permute-start.3 = (bf16[16,8,1024]{2,1,0:T(8,128)(2,1)}, bf16[16,8,1024]{2,1,0:T(8,128)(2,1)S(1)}, u32[]{:S(2)}, u32[]{:S(2)}) collective-permute-start(bf16[16,8,1024]{2,1,0:T(8,128)(2,1)} %get-tuple-element.344), channel_id=1, source_target_pairs={{0,30},{2,0},{4,2},{6,4},{8,6},{10,8},{12,10},{14,12},{16,14},{18,... | collective-permute-start | bytes 786440 | tf_op jit(solution)/shard_map/ppermute | solution.py:36
  44.0 7.8 %collective-permute-done.2 = bf16[16,8,1024]{2,1,0:T(8,128)(2,1)S(1)} collective-permute-done((bf16[16,8,1024]{2,1,0:T(8,128)(2,1)}, bf16[16,8,1024]{2,1,0:T(8,128)(2,1)S(1)}, u32[]{:S(2)}, u32[]{:S(2)}) %collective-permute-start.2) | collective-permute-done | bytes 262176 | tf_op jit(solution)/shard_map/ppermute | solution.py:28
  54.2 3.2 collective-permute-start.5
  57.4 7.4 %collective-permute-done.4 = bf16[16,8,1024]{2,1,0:T(8,128)(2,1)S(1)} collective-permute-done((bf16[16,8,1024]{2,1,0:T(8,128)(2,1)S(1)}, bf16[16,8,1024]{2,1,0:T(8,128)(2,1)S(1)}, u32[]{:S(2)}, u32[]{:S(2)}) %collective-permute-start.4) | collective-permute-done | bytes 262176 | tf_op jit(solution)/shard_map/ppermute | solution.py:28
  67.4 3.1 collective-permute-start.7
  70.5 6.6 %collective-permute-done.6 = bf16[16,8,1024]{2,1,0:T(8,128)(2,1)S(1)} collective-permute-done((bf16[16,8,1024]{2,1,0:T(8,128)(2,1)S(1)}, bf16[16,8,1024]{2,1,0:T(8,128)(2,1)S(1)}, u32[]{:S(2)}, u32[]{:S(2)}) %collective-permute-start.6) | collective-permute-done | bytes 262176 | tf_op jit(solution)/shard_map/ppermute | solution.py:28
  80.3 3.8 %collective-permute-start.9 = (bf16[16,8,1024]{2,1,0:T(8,128)(2,1)S(1)}, bf16[16,8,1024]{2,1,0:T(8,128)(2,1)S(1)}, u32[]{:S(2)}, u32[]{:S(2)}) collective-permute-start(bf16[16,8,1024]{2,1,0:T(8,128)(2,1)S(1)} %collective-permute-done.7), channel_id=1, source_target_pairs={{0,30},{2,0},{4,2},{6,4},{8,6},{10,8},{12,10},{14,12},{16,14},{18,... | collective-permute-start | bytes 786440 | tf_op jit(solution)/shard_map/ppermute | solution.py:36
  84.9 6.3 %collective-permute-done.8 = bf16[16,8,1024]{2,1,0:T(8,128)(2,1)S(1)} collective-permute-done((bf16[16,8,1024]{2,1,0:T(8,128)(2,1)S(1)}, bf16[16,8,1024]{2,1,0:T(8,128)(2,1)S(1)}, u32[]{:S(2)}, u32[]{:S(2)}) %collective-permute-start.8) | collective-permute-done | bytes 262176 | tf_op jit(solution)/shard_map/ppermute | solution.py:28
  95.1 3.2 collective-permute-start.11
  99.0 5.8 %collective-permute-done.10 = bf16[16,8,1024]{2,1,0:T(8,128)(2,1)S(1)} collective-permute-done((bf16[16,8,1024]{2,1,0:T(8,128)(2,1)S(1)}, bf16[16,8,1024]{2,1,0:T(8,128)(2,1)S(1)}, u32[]{:S(2)}, u32[]{:S(2)}) %collective-permute-start.10) | collective-permute-done | bytes 262176 | tf_op jit(solution)/shard_map/ppermute | solution.py:28
  108.7 3.1 collective-permute-start.13
  112.6 6.7 %collective-permute-done.12 = bf16[16,8,1024]{2,1,0:T(8,128)(2,1)S(1)} collective-permute-done((bf16[16,8,1024]{2,1,0:T(8,128)(2,1)S(1)}, bf16[16,8,1024]{2,1,0:T(8,128)(2,1)S(1)}, u32[]{:S(2)}, u32[]{:S(2)}) %collective-permute-start.12) | collective-permute-done | bytes 262176 | tf_op jit(solution)/shard_map/ppermute | solution.py:28
  123.3 3.1 collective-permute-start.15
  127.1 5.1 %collective-permute-done.14 = bf16[16,8,1024]{2,1,0:T(8,128)(2,1)S(1)} collective-permute-done((bf16[16,8,1024]{2,1,0:T(8,128)(2,1)S(1)}, bf16[16,8,1024]{2,1,0:T(8,128)(2,1)S(1)}, u32[]{:S(2)}, u32[]{:S(2)}) %collective-permute-start.14) | collective-permute-done | bytes 262176 | tf_op jit(solution)/shard_map/ppermute | solution.py:28
  137.0 5.3 %collective-permute-done.16 = bf16[16,8,1024]{2,1,0:T(8,128)(2,1)S(1)} collective-permute-done((bf16[16,8,1024]{2,1,0:T(8,128)(2,1)S(1)}, bf16[16,8,1024]{2,1,0:T(8,128)(2,1)S(1)}, u32[]{:S(2)}, u32[]{:S(2)}) %collective-permute-start.16) | collective-permute-done | bytes 262176 | tf_op jit(solution)/shard_map/ppermute | solution.py:28
  143.0 11.8 %copy.12 = bf16[4,64,8,1024]{1,2,3,0:T(8,128)(2,1)} copy(bf16[4,64,8,1024]{3,2,1,0:T(8,128)(2,1)} %bitcast.11) | data formatting | bytes 8388608
  155.7 108.4 %while.17 = (s32[]{:T(128)}, f32[128,1024]{1,0:T(8,128)}, s32[]{:T(128)}, s32[16,256]{1,0:T(8,128)S(1)}, bf16[4,64,8,1024]{1,2,3,0:T(8,128)(2,1)}, /*index=5*/bf16[16,8,1024]{2,1,0:T(8,128)(2,1)}, s32[]{:T(128)}, s32[]{:T(128)}) while((s32[]{:T(128)}, f32[128,1024]{1,0:T(8,128)}, s32[]{:T(128)}, s32[16,256]{1,0:T(8,128)S(1)}, ...), condition=%wide.region_3.4_spmd.clone, body=%wide.region_0.3_spmd.clone.sunk | while | flops 312674400 | bytes 18896416 | solution.py:173
  155.7 27.1 %conditional.3 = (f32[128,1024]{1,0:T(8,128)}) conditional(s32[]{:T(128)} %convert_element_type.47, f32[128,1024]{1,0:T(8,128)} %get-tuple-element.348, (s32[]{:T(128)}, s32[1,64]{1,0:T(1,128)S(1)}, s32[]{:T(128)}, s32[16]{0:T(128)S(1)}, s32[16,256]{1,0:T(8,128)S(1)}, /*index=5*/s32[]{:T(128)}, bf16[4,64,8,1024]{1,2,3,0:T(8,128)(2,1)}, ...), branch_computations={%region_1.1_spmd, %region_2.2_spmd} | conditional | flops 312674400 | bytes 18895900 | solution.py:166
  159.4 3.7 %copy.8 = bf16[16,16,512]{1,0,2:T(8,128)(2,1)} copy(bf16[16,16,512]{2,1,0:T(8,128)(2,1)} %get-tuple-element.286) | data formatting | bytes 524288 | tf_op jit(solution)/shard_map/while/body/eval_jaxpr/cond/branch_1_fun/concatenate | solution.py:95
  163.0 4.2 %convert_bitcast_fusion.1 = bf16[16,64,512]{1,0,2:T(8,128)(2,1)} fusion(bf16[16,16,512]{1,0,2:T(8,128)(2,1)} %copy.8, bf16[64,8,512]{0,1,2:T(8,128)(2,1)S(1)} %get-tuple-element.281, bf16[64,8,512]{0,1,2:T(8,128)(2,1)S(1)} %get-tuple-element.282), kind=kOutput, calls=%fused_computation.14 | convolution fusion | flops 19398656 | bytes 2359296 | tf_op jit(solution)/shard_map/while/body/eval_jaxpr/cond/branch_1_fun/asf,bsf->abf/dot_general | solution.py:99
  167.2 3.3 copy.9
  170.5 2.8 copy.10
  173.3 4.2 %convert_bitcast_fusion = bf16[16,64,512]{1,0,2:T(8,128)(2,1)} fusion(bf16[16,16,512]{1,0,2:T(8,128)(2,1)} %copy.10, bf16[64,8,512]{0,1,2:T(8,128)(2,1)S(1)} %get-tuple-element.282, bf16[64,8,512]{0,1,2:T(8,128)(2,1)S(1)} %get-tuple-element.281), kind=kOutput, calls=%fused_computation.13 | convolution fusion | flops 19398656 | bytes 2359296 | tf_op jit(solution)/shard_map/while/body/eval_jaxpr/cond/branch_1_fun/asf,bsf->abf/dot_general | solution.py:101
  180.2 2.6 fusion.18
  182.8 27.1 %conditional.3 = (f32[128,1024]{1,0:T(8,128)}) conditional(s32[]{:T(128)} %convert_element_type.47, f32[128,1024]{1,0:T(8,128)} %get-tuple-element.348, (s32[]{:T(128)}, s32[1,64]{1,0:T(1,128)S(1)}, s32[]{:T(128)}, s32[16]{0:T(128)S(1)}, s32[16,256]{1,0:T(8,128)S(1)}, /*index=5*/s32[]{:T(128)}, bf16[4,64,8,1024]{1,2,3,0:T(8,128)(2,1)}, ...), branch_computations={%region_1.1_spmd, %region_2.2_spmd} | conditional | flops 312674400 | bytes 18895900 | solution.py:166
  186.5 3.7 %copy.8 = bf16[16,16,512]{1,0,2:T(8,128)(2,1)} copy(bf16[16,16,512]{2,1,0:T(8,128)(2,1)} %get-tuple-element.286) | data formatting | bytes 524288 | tf_op jit(solution)/shard_map/while/body/eval_jaxpr/cond/branch_1_fun/concatenate | solution.py:95
  190.1 4.2 %convert_bitcast_fusion.1 = bf16[16,64,512]{1,0,2:T(8,128)(2,1)} fusion(bf16[16,16,512]{1,0,2:T(8,128)(2,1)} %copy.8, bf16[64,8,512]{0,1,2:T(8,128)(2,1)S(1)} %get-tuple-element.281, bf16[64,8,512]{0,1,2:T(8,128)(2,1)S(1)} %get-tuple-element.282), kind=kOutput, calls=%fused_computation.14 | convolution fusion | flops 19398656 | bytes 2359296 | tf_op jit(solution)/shard_map/while/body/eval_jaxpr/cond/branch_1_fun/asf,bsf->abf/dot_general | solution.py:99
  194.3 3.3 copy.9
  197.6 2.8 copy.10
  200.4 4.2 %convert_bitcast_fusion = bf16[16,64,512]{1,0,2:T(8,128)(2,1)} fusion(bf16[16,16,512]{1,0,2:T(8,128)(2,1)} %copy.10, bf16[64,8,512]{0,1,2:T(8,128)(2,1)S(1)} %get-tuple-element.282, bf16[64,8,512]{0,1,2:T(8,128)(2,1)S(1)} %get-tuple-element.281), kind=kOutput, calls=%fused_computation.13 | convolution fusion | flops 19398656 | bytes 2359296 | tf_op jit(solution)/shard_map/while/body/eval_jaxpr/cond/branch_1_fun/asf,bsf->abf/dot_general | solution.py:101
  209.9 27.1 %conditional.3 = (f32[128,1024]{1,0:T(8,128)}) conditional(s32[]{:T(128)} %convert_element_type.47, f32[128,1024]{1,0:T(8,128)} %get-tuple-element.348, (s32[]{:T(128)}, s32[1,64]{1,0:T(1,128)S(1)}, s32[]{:T(128)}, s32[16]{0:T(128)S(1)}, s32[16,256]{1,0:T(8,128)S(1)}, /*index=5*/s32[]{:T(128)}, bf16[4,64,8,1024]{1,2,3,0:T(8,128)(2,1)}, ...), branch_computations={%region_1.1_spmd, %region_2.2_spmd} | conditional | flops 312674400 | bytes 18895900 | solution.py:166
  213.6 3.7 %copy.8 = bf16[16,16,512]{1,0,2:T(8,128)(2,1)} copy(bf16[16,16,512]{2,1,0:T(8,128)(2,1)} %get-tuple-element.286) | data formatting | bytes 524288 | tf_op jit(solution)/shard_map/while/body/eval_jaxpr/cond/branch_1_fun/concatenate | solution.py:95
  217.3 4.2 %convert_bitcast_fusion.1 = bf16[16,64,512]{1,0,2:T(8,128)(2,1)} fusion(bf16[16,16,512]{1,0,2:T(8,128)(2,1)} %copy.8, bf16[64,8,512]{0,1,2:T(8,128)(2,1)S(1)} %get-tuple-element.281, bf16[64,8,512]{0,1,2:T(8,128)(2,1)S(1)} %get-tuple-element.282), kind=kOutput, calls=%fused_computation.14 | convolution fusion | flops 19398656 | bytes 2359296 | tf_op jit(solution)/shard_map/while/body/eval_jaxpr/cond/branch_1_fun/asf,bsf->abf/dot_general | solution.py:99
  221.4 3.3 copy.9
  224.7 2.8 copy.10
  227.5 4.2 %convert_bitcast_fusion = bf16[16,64,512]{1,0,2:T(8,128)(2,1)} fusion(bf16[16,16,512]{1,0,2:T(8,128)(2,1)} %copy.10, bf16[64,8,512]{0,1,2:T(8,128)(2,1)S(1)} %get-tuple-element.282, bf16[64,8,512]{0,1,2:T(8,128)(2,1)S(1)} %get-tuple-element.281), kind=kOutput, calls=%fused_computation.13 | convolution fusion | flops 19398656 | bytes 2359296 | tf_op jit(solution)/shard_map/while/body/eval_jaxpr/cond/branch_1_fun/asf,bsf->abf/dot_general | solution.py:101
  237.0 27.1 %conditional.3 = (f32[128,1024]{1,0:T(8,128)}) conditional(s32[]{:T(128)} %convert_element_type.47, f32[128,1024]{1,0:T(8,128)} %get-tuple-element.348, (s32[]{:T(128)}, s32[1,64]{1,0:T(1,128)S(1)}, s32[]{:T(128)}, s32[16]{0:T(128)S(1)}, s32[16,256]{1,0:T(8,128)S(1)}, /*index=5*/s32[]{:T(128)}, bf16[4,64,8,1024]{1,2,3,0:T(8,128)(2,1)}, ...), branch_computations={%region_1.1_spmd, %region_2.2_spmd} | conditional | flops 312674400 | bytes 18895900 | solution.py:166
  240.7 3.7 %copy.8 = bf16[16,16,512]{1,0,2:T(8,128)(2,1)} copy(bf16[16,16,512]{2,1,0:T(8,128)(2,1)} %get-tuple-element.286) | data formatting | bytes 524288 | tf_op jit(solution)/shard_map/while/body/eval_jaxpr/cond/branch_1_fun/concatenate | solution.py:95
  244.4 4.2 %convert_bitcast_fusion.1 = bf16[16,64,512]{1,0,2:T(8,128)(2,1)} fusion(bf16[16,16,512]{1,0,2:T(8,128)(2,1)} %copy.8, bf16[64,8,512]{0,1,2:T(8,128)(2,1)S(1)} %get-tuple-element.281, bf16[64,8,512]{0,1,2:T(8,128)(2,1)S(1)} %get-tuple-element.282), kind=kOutput, calls=%fused_computation.14 | convolution fusion | flops 19398656 | bytes 2359296 | tf_op jit(solution)/shard_map/while/body/eval_jaxpr/cond/branch_1_fun/asf,bsf->abf/dot_general | solution.py:99
  248.5 3.3 copy.9
  251.8 2.8 copy.10
  254.6 4.2 %convert_bitcast_fusion = bf16[16,64,512]{1,0,2:T(8,128)(2,1)} fusion(bf16[16,16,512]{1,0,2:T(8,128)(2,1)} %copy.10, bf16[64,8,512]{0,1,2:T(8,128)(2,1)S(1)} %get-tuple-element.282, bf16[64,8,512]{0,1,2:T(8,128)(2,1)S(1)} %get-tuple-element.281), kind=kOutput, calls=%fused_computation.13 | convolution fusion | flops 19398656 | bytes 2359296 | tf_op jit(solution)/shard_map/while/body/eval_jaxpr/cond/branch_1_fun/asf,bsf->abf/dot_general | solution.py:101
  264.2 9.8 %cosine_multiply_fusion = (f32[512,1024]{1,0:T(8,128)S(1)}, f32[512,1024]{1,0:T(8,128)}) fusion(s32[1024]{0:T(1024)S(1)} %iota_add_fusion, s32[512]{0:T(512)S(1)} %iota_add_fusion.2, f32[512]{0:T(512)S(1)} %get-tuple-element.298, f32[512]{0:T(512)S(1)} %get-tuple-element.299), kind=kLoop, calls=%fused_computation.55 | loop fusion | flops 8388608 | bytes 4204544 | tf_op jit(solution)/shard_map/mul | solution.py:70
  274.0 62.8 %reduce-scatter.3.cloned.1.call-done = f32[8,1024]{1,0:T(8,128)} async-done(((f32[128,1024]{1,0:T(8,128)}), f32[8,1024]{1,0:T(8,128)}) %reduce-scatter.3.cloned.1.call-update) | async-done | bytes 32784 | tf_op jit(solution)/shard_map/reduce_scatter | solution.py:175
  336.9 4.3 %fusion.32 = f32[8,1024]{1,0:T(8,128)} fusion(f32[8,1024]{1,0:T(8,128)} %reduce-scatter.3.cloned.1.call-done, f32[512,1024]{1,0:T(8,128)} %get-tuple-element.295, f32[512,1024]{1,0:T(8,128)S(1)} %get-tuple-element.294), kind=kOutput, calls=%fused_computation.38 | convolution fusion | flops 101711872 | bytes 4259840 | tf_op jit(solution)/shard_map/dot_general | solution.py:176
  341.2 3.9 %reduce-scatter.5.cloned.1.call-done = f32[8,512]{1,0:T(8,128)} async-done(((f32[8,1024]{1,0:T(8,128)}), f32[8,512]{1,0:T(8,128)}) %reduce-scatter.5.cloned.1.call-update) | async-done | bytes 16400 | tf_op jit(solution)/shard_map/reduce_scatter | solution.py:179
  (99 shorter events, 74.2 us)
Async XLA Ops:
  6.5 16.7 %copy-start = (f32[16,8,2048]{2,1,0:T(8,128)S(1)}, f32[16,8,2048]{2,1,0:T(8,128)}, u32[]{:S(2)}) copy-start(f32[16,8,2048]{2,1,0:T(8,128)} %param.6) | copy-start | bytes 3145732
  6.5 330.3 %reduce-scatter.3.cloned.1.call-start = ((), (), s32[]{:S(2)}) async-start(), calls=%async_computation.2 | async-start | bytes 557056 | tf_op jit(solution)/shard_map/reduce_scatter | solution.py:175
  28.1 3.7 %collective-permute-start = (f32[16,8,32]{2,1,0:T(8,128)S(1)}, f32[16,8,32]{2,1,0:T(8,128)S(1)}, u32[]{:S(2)}, u32[]{:S(2)}) collective-permute-start(f32[16,8,32]{2,1,0:T(8,128)S(1)} %get-tuple-element.292), channel_id=1, source_target_pairs={{0,1},{2,3},{4,5},{6,7},{8,9},{10,11},{12,13},{14,15},{16,17},{18,... | collective-permute-start | bytes 49160 | tf_op jit(solution)/shard_map/ppermute | solution.py:48
  30.5 3.1 collective-permute-start.1
  37.7 14.1 %collective-permute-start.2 = (bf16[16,8,1024]{2,1,0:T(8,128)(2,1)}, bf16[16,8,1024]{2,1,0:T(8,128)(2,1)S(1)}, u32[]{:S(2)}, u32[]{:S(2)}) collective-permute-start(bf16[16,8,1024]{2,1,0:T(8,128)(2,1)} %get-tuple-element.344), channel_id=1, source_target_pairs={{0,2},{2,4},{4,6},{6,8},{8,10},{10,12},{12,14},{14,16},{16,18},{18... | collective-permute-start | bytes 786440 | tf_op jit(solution)/shard_map/ppermute | solution.py:28
  40.0 14.2 %collective-permute-start.3 = (bf16[16,8,1024]{2,1,0:T(8,128)(2,1)}, bf16[16,8,1024]{2,1,0:T(8,128)(2,1)S(1)}, u32[]{:S(2)}, u32[]{:S(2)}) collective-permute-start(bf16[16,8,1024]{2,1,0:T(8,128)(2,1)} %get-tuple-element.344), channel_id=1, source_target_pairs={{0,30},{2,0},{4,2},{6,4},{8,6},{10,8},{12,10},{14,12},{16,14},{18,... | collective-permute-start | bytes 786440 | tf_op jit(solution)/shard_map/ppermute | solution.py:36
  51.8 13.0 %collective-permute-start.4 = (bf16[16,8,1024]{2,1,0:T(8,128)(2,1)S(1)}, bf16[16,8,1024]{2,1,0:T(8,128)(2,1)S(1)}, u32[]{:S(2)}, u32[]{:S(2)}) collective-permute-start(bf16[16,8,1024]{2,1,0:T(8,128)(2,1)S(1)} %collective-permute-done.2), channel_id=1, source_target_pairs={{0,2},{2,4},{4,6},{6,8},{8,10},{10,12},{12,14},{14,16},{16,18},{18... | collective-permute-start | bytes 786440 | tf_op jit(solution)/shard_map/ppermute | solution.py:28
  54.2 13.2 %collective-permute-start.5 = (bf16[16,8,1024]{2,1,0:T(8,128)(2,1)S(1)}, bf16[16,8,1024]{2,1,0:T(8,128)(2,1)S(1)}, u32[]{:S(2)}, u32[]{:S(2)}) collective-permute-start(bf16[16,8,1024]{2,1,0:T(8,128)(2,1)S(1)} %collective-permute-done.3), channel_id=1, source_target_pairs={{0,30},{2,0},{4,2},{6,4},{8,6},{10,8},{12,10},{14,12},{16,14},{18,... | collective-permute-start | bytes 786440 | tf_op jit(solution)/shard_map/ppermute | solution.py:36
  64.9 12.2 %collective-permute-start.6 = (bf16[16,8,1024]{2,1,0:T(8,128)(2,1)S(1)}, bf16[16,8,1024]{2,1,0:T(8,128)(2,1)S(1)}, u32[]{:S(2)}, u32[]{:S(2)}) collective-permute-start(bf16[16,8,1024]{2,1,0:T(8,128)(2,1)S(1)} %collective-permute-done.4), channel_id=1, source_target_pairs={{0,2},{2,4},{4,6},{6,8},{8,10},{10,12},{12,14},{14,16},{16,18},{18... | collective-permute-start | bytes 786440 | tf_op jit(solution)/shard_map/ppermute | solution.py:28
  67.4 13.0 %collective-permute-start.7 = (bf16[16,8,1024]{2,1,0:T(8,128)(2,1)S(1)}, bf16[16,8,1024]{2,1,0:T(8,128)(2,1)S(1)}, u32[]{:S(2)}, u32[]{:S(2)}) collective-permute-start(bf16[16,8,1024]{2,1,0:T(8,128)(2,1)S(1)} %collective-permute-done.5), channel_id=1, source_target_pairs={{0,30},{2,0},{4,2},{6,4},{8,6},{10,8},{12,10},{14,12},{16,14},{18,... | collective-permute-start | bytes 786440 | tf_op jit(solution)/shard_map/ppermute | solution.py:36
  77.1 14.1 %collective-permute-start.8 = (bf16[16,8,1024]{2,1,0:T(8,128)(2,1)S(1)}, bf16[16,8,1024]{2,1,0:T(8,128)(2,1)S(1)}, u32[]{:S(2)}, u32[]{:S(2)}) collective-permute-start(bf16[16,8,1024]{2,1,0:T(8,128)(2,1)S(1)} %collective-permute-done.6), channel_id=1, source_target_pairs={{0,2},{2,4},{4,6},{6,8},{8,10},{10,12},{12,14},{14,16},{16,18},{18... | collective-permute-start | bytes 786440 | tf_op jit(solution)/shard_map/ppermute | solution.py:28
  80.3 14.8 %collective-permute-start.9 = (bf16[16,8,1024]{2,1,0:T(8,128)(2,1)S(1)}, bf16[16,8,1024]{2,1,0:T(8,128)(2,1)S(1)}, u32[]{:S(2)}, u32[]{:S(2)}) collective-permute-start(bf16[16,8,1024]{2,1,0:T(8,128)(2,1)S(1)} %collective-permute-done.7), channel_id=1, source_target_pairs={{0,30},{2,0},{4,2},{6,4},{8,6},{10,8},{12,10},{14,12},{16,14},{18,... | collective-permute-start | bytes 786440 | tf_op jit(solution)/shard_map/ppermute | solution.py:36
  91.2 13.6 %collective-permute-start.10 = (bf16[16,8,1024]{2,1,0:T(8,128)(2,1)S(1)}, bf16[16,8,1024]{2,1,0:T(8,128)(2,1)S(1)}, u32[]{:S(2)}, u32[]{:S(2)}) collective-permute-start(bf16[16,8,1024]{2,1,0:T(8,128)(2,1)S(1)} %collective-permute-done.8), channel_id=1, source_target_pairs={{0,2},{2,4},{4,6},{6,8},{8,10},{10,12},{12,14},{14,16},{16,18},{18... | collective-permute-start | bytes 786440 | tf_op jit(solution)/shard_map/ppermute | solution.py:28
  95.1 13.6 %collective-permute-start.11 = (bf16[16,8,1024]{2,1,0:T(8,128)(2,1)S(1)}, bf16[16,8,1024]{2,1,0:T(8,128)(2,1)S(1)}, u32[]{:S(2)}, u32[]{:S(2)}) collective-permute-start(bf16[16,8,1024]{2,1,0:T(8,128)(2,1)S(1)} %collective-permute-done.9), channel_id=1, source_target_pairs={{0,30},{2,0},{4,2},{6,4},{8,6},{10,8},{12,10},{14,12},{16,14},{18,... | collective-permute-start | bytes 786440 | tf_op jit(solution)/shard_map/ppermute | solution.py:36
  104.8 14.5 %collective-permute-start.12 = (bf16[16,8,1024]{2,1,0:T(8,128)(2,1)S(1)}, bf16[16,8,1024]{2,1,0:T(8,128)(2,1)S(1)}, u32[]{:S(2)}, u32[]{:S(2)}) collective-permute-start(bf16[16,8,1024]{2,1,0:T(8,128)(2,1)S(1)} %collective-permute-done.10), channel_id=1, source_target_pairs={{0,2},{2,4},{4,6},{6,8},{8,10},{10,12},{12,14},{14,16},{16,18},{18... | collective-permute-start | bytes 786440 | tf_op jit(solution)/shard_map/ppermute | solution.py:28
  108.7 14.5 %collective-permute-start.13 = (bf16[16,8,1024]{2,1,0:T(8,128)(2,1)S(1)}, bf16[16,8,1024]{2,1,0:T(8,128)(2,1)S(1)}, u32[]{:S(2)}, u32[]{:S(2)}) collective-permute-start(bf16[16,8,1024]{2,1,0:T(8,128)(2,1)S(1)} %collective-permute-done.11), channel_id=1, source_target_pairs={{0,30},{2,0},{4,2},{6,4},{8,6},{10,8},{12,10},{14,12},{16,14},{18,... | collective-permute-start | bytes 786440 | tf_op jit(solution)/shard_map/ppermute | solution.py:36
  119.3 12.9 %collective-permute-start.14 = (bf16[16,8,1024]{2,1,0:T(8,128)(2,1)S(1)}, bf16[16,8,1024]{2,1,0:T(8,128)(2,1)S(1)}, u32[]{:S(2)}, u32[]{:S(2)}) collective-permute-start(bf16[16,8,1024]{2,1,0:T(8,128)(2,1)S(1)} %collective-permute-done.12), channel_id=1, source_target_pairs={{0,2},{2,4},{4,6},{6,8},{8,10},{10,12},{12,14},{14,16},{16,18},{18... | collective-permute-start | bytes 786440 | tf_op jit(solution)/shard_map/ppermute | solution.py:28
  123.3 13.0 %collective-permute-start.15 = (bf16[16,8,1024]{2,1,0:T(8,128)(2,1)S(1)}, bf16[16,8,1024]{2,1,0:T(8,128)(2,1)S(1)}, u32[]{:S(2)}, u32[]{:S(2)}) collective-permute-start(bf16[16,8,1024]{2,1,0:T(8,128)(2,1)S(1)} %collective-permute-done.13), channel_id=1, source_target_pairs={{0,30},{2,0},{4,2},{6,4},{8,6},{10,8},{12,10},{14,12},{16,14},{18,... | collective-permute-start | bytes 786440 | tf_op jit(solution)/shard_map/ppermute | solution.py:36
  132.3 10.0 %collective-permute-start.16 = (bf16[16,8,1024]{2,1,0:T(8,128)(2,1)S(1)}, bf16[16,8,1024]{2,1,0:T(8,128)(2,1)S(1)}, u32[]{:S(2)}, u32[]{:S(2)}) collective-permute-start(bf16[16,8,1024]{2,1,0:T(8,128)(2,1)S(1)} %collective-permute-done.14), channel_id=1, source_target_pairs={{0,2},{2,4},{4,6},{6,8},{8,10},{10,12},{12,14},{14,16},{16,18},{18... | collective-permute-start | bytes 786440 | tf_op jit(solution)/shard_map/ppermute | solution.py:28
  143.0 12.7 %copy-start.1 = (s32[16,256]{1,0:T(8,128)S(1)}, s32[16,256]{1,0:T(8,128)}, u32[]{:S(2)}) copy-start(s32[16,256]{1,0:T(8,128)} %param.7) | copy-start | bytes 49156
  264.2 80.9 %reduce-scatter.5.cloned.1.call-start = ((), (), s32[]{:S(2)}) async-start(), calls=%async_computation.3 | async-start | bytes 49152 | tf_op jit(solution)/shard_map/reduce_scatter | solution.py:179
Sparse Core Ops, SparseCore 0:
  264.3 72.5 reduce-scatter.2
  341.3 3.7 reduce-scatter.4
